TPU v7x, 512 devices: a whole 4x8x8 slice. The times are simulated.
512 devices in a mesh: dp: 64 (over x, z, y_lo), tp: 8 (over y_hi, core).
Axes of the slice: x: 4, y: 8 (y_hi: 4, y_lo: 2; y = y_hi * 2 + y_lo), z: 8, core: 2. Of those that a mesh axis runs over, the one named last changes fastest.
Arguments:
- stash_values: bfloat16 [65536, 8192], P(('dp', 'tp')), may hold values from -127 to 127
- stash_scales: bfloat16 [65536, 64], P(('dp', 'tp')), may hold values from 0.001 to 0.13
- value_grad: bfloat16 [65536, 1024], P('dp', 'tp'), may hold values from -19 to 19
Outputs:
- clipped_grad: float32 [8192, 1024], P('dp', 'tp')
All inputs are finite; a program needn't handle non-finite values.
Results may differ from a plain program's by a relative error of at most 0.0019.
Values may be sent and summed in bfloat16 or wider, within the bound.
A program may use at most 64 MiB of HBM per device.

v0:
```python
import jax
import jax.numpy as jnp
from jax import lax
from jax.sharding import Mesh
from jax.sharding import PartitionSpec as P

DP = ("dp_0", "dp_1", "dp_2")
TP = ("tp_0", "tp_1")
DP_TP = ("dp_0", "dp_1", "dp_2", "tp_0", "tp_1")


def copy_for_each(shard, axis):
    copies = jnp.broadcast_to(shard, (lax.axis_size(axis), *shard.shape))
    return lax.all_to_all(copies, axis, split_axis=0, concat_axis=0, tiled=True)


def in_order(pieces, dim):
    pieces = jnp.moveaxis(pieces, 0, dim)
    shape = pieces.shape
    return pieces.reshape(*shape[:dim], shape[dim] * shape[dim + 1], *shape[dim + 2 :])


def collect(shard, axis, dim):
    pieces = copy_for_each(shard, axis)
    return in_order(pieces, dim)


def split_up(shard, dim, size):
    shape = shard.shape
    pieces = shard.reshape(*shape[:dim], size, shape[dim] // size, *shape[dim + 1 :])
    return jnp.moveaxis(pieces, dim, 0)


def sent_and_summed(shard, axis, dim):
    pieces = split_up(shard, dim, lax.axis_size(axis))
    arrived = lax.all_to_all(pieces, axis, split_axis=0, concat_axis=0, tiled=True)
    return arrived.astype(jnp.float32).sum(axis=0)


def over_axes(shard, axes):
    for axis in axes:
        shard = lax.psum(shard, axis)
    return shard


def block_dequantize(values, scales):
    rows = values.shape[0]
    blocks = scales.shape[1]
    scaled = (
        values.astype(jnp.float32).reshape(rows, blocks, values.shape[1] // blocks)
        * scales.astype(jnp.float32)[:, :, None]
    )
    return scaled.reshape(rows, values.shape[1]).astype(jnp.bfloat16)


def body(stash_values, stash_scales, value_grad):
    width = stash_values.shape[1]
    columns = value_grad.shape[1]
    dp_count = lax.axis_size(DP)
    tp_count = lax.axis_size(TP)
    own_tokens = stash_values.shape[0]
    sub_rows = width // (dp_count * tp_count)
    inputs = block_dequantize(stash_values, stash_scales)
    inputs = inputs.reshape(own_tokens, dp_count, tp_count, sub_rows)
    features = lax.all_to_all(inputs, TP, split_axis=2, concat_axis=0, tiled=True)
    features = features.reshape(own_tokens * tp_count, dp_count * sub_rows)
    all_heads = lax.dot_general(
        features,
        collect(value_grad, TP, 1),
        (((0,), (0,)), ((), ())),
        preferred_element_type=jnp.float32,
    )
    summed = sent_and_summed(all_heads.astype(jnp.bfloat16), DP, 0)
    local = lax.all_to_all(summed, TP, split_axis=1, concat_axis=0, tiled=True)
    total = over_axes(jnp.sum(summed * summed), DP_TP)
    limit = jnp.sqrt(jnp.float32(width * columns * lax.axis_size(TP)))
    return local * jnp.minimum(jnp.float32(1.0), limit / jnp.sqrt(total))


def solution(mesh):
    torus = Mesh(mesh.devices.reshape(4, 8, 2, 4, 2), ("dp_0", "dp_1", "dp_2", "tp_0", "tp_1"))
    return jax.shard_map(
        body,
        mesh=torus,
        in_specs=(P(DP_TP, None), P(DP_TP, None), P(DP, TP)),
        out_specs=P(DP, TP),
        check_vma=False,
    )
```

profile of v0, /device:TPU:1, one launch (start us, length us, event | category | flops | bytes accessed | tf_op | source)
XLA Modules:
  0.0 247.4 jit_solution(15634709426231722610)
XLA Ops:
  0.0 0.7 convert_element_type.16
  0.7 3.2 %copy.12 = bf16[128,8192]{0,1:T(8,128)(2,1)S(1)} copy(bf16[128,8192]{1,0:T(8,128)(2,1)} %param.3) | data formatting | bytes 4194304 | tf_op args[0]
  3.9 0.4 fusion
  4.4 1.7 copy.13
  6.1 0.0 copy-start
  6.1 10.5 %all-to-all-start = ((bf16[128,64,8,16]{0,3,1,2:T(8,128)(2,1)}), bf16[128,64,8,16]{0,3,1,2:T(8,128)(2,1)S(1)}, u32[]{:S(2)}, u32[]{:S(2)}) async-start(bf16[128,64,8,16]{0,3,1,2:T(8,128)(2,1)} %copy.13), calls=%async_computation | async-start | bytes 4194304 | tf_op jit(solution)/shard_map/all_to_all | solution.py:65
  16.6 0.0 copy-done
  16.6 0.1 copy.15
  16.7 48.7 %all-to-all-done = bf16[128,64,8,16]{0,3,1,2:T(8,128)(2,1)S(1)} async-done(((bf16[128,64,8,16]{0,3,1,2:T(8,128)(2,1)}), bf16[128,64,8,16]{0,3,1,2:T(8,128)(2,1)S(1)}, u32[]{:S(2)}, u32[]{:S(2)}) %all-to-all-start) | async-done | bytes 2097184 | tf_op jit(solution)/shard_map/all_to_all | solution.py:65
  65.4 1.6 broadcast_in_dim.4
  67.0 5.0 %all-to-all-start.1 = ((bf16[8,1024,128]{1,2,0:T(8,128)(2,1)}), bf16[8,1024,128]{1,2,0:T(8,128)(2,1)}, u32[]{:S(2)}, u32[]{:S(2)}) async-start(bf16[8,1024,128]{1,2,0:T(8,128)(2,1)} %broadcast_in_dim.4), calls=%async_computation.1 | async-start | bytes 4194304 | tf_op jit(solution)/shard_map/all_to_all | solution.py:14
  71.9 3.8 %copy.14 = bf16[8,128,64,1,16]{1,0,4,2,3:T(8,128)(2,1)} copy(bf16[8,128,64,1,16]{1,4,2,0,3:T(8,128)(2,1)S(1)} %bitcast.30) | data formatting | bytes 4194304 | tf_op jit(solution)/shard_map/all_to_all | solution.py:65
  75.7 33.4 %all-to-all-done.1 = bf16[8,1024,128]{1,2,0:T(8,128)(2,1)} async-done(((bf16[8,1024,128]{1,2,0:T(8,128)(2,1)}), bf16[8,1024,128]{1,2,0:T(8,128)(2,1)}, u32[]{:S(2)}, u32[]{:S(2)}) %all-to-all-start.1) | async-done | bytes 2097184 | tf_op jit(solution)/shard_map/all_to_all | solution.py:14
  109.1 4.6 %fusion.4 = bf16[1024,1024]{1,0:T(8,128)(2,1)S(1)} fusion(bf16[1024,1024]{0,1:T(8,128)(2,1)} %bitcast.5, bf16[128,8,8,128]{3,2,1,0:T(8,128)(2,1)} %bitcast.32), kind=kOutput, calls=%fused_computation.6 | convolution fusion | flops 2148532224 | bytes 6291456 | tf_op jit(solution)/shard_map/dot_general | solution.py:67
  113.7 75.6 %all_to_all.38 = bf16[64,16,1024]{2,1,0:T(8,128)(2,1)S(1)} all-to-all(bf16[64,16,1024]{2,1,0:T(8,128)(2,1)S(1)} %bitcast.33), channel_id=1, replica_groups=mesh['dp_0'=4,'dp_1'=8,'dp_2'=2,'tp_0'=4,'tp_1'=2] {'dp_0','dp_1','dp_2'}, dimensions={0} | all-to-all | bytes 4194304 | tf_op jit(solution)/shard_map/all_to_all | solution.py:36
  189.2 0.4 convert_reduce_fusion
  189.6 0.6 copy_bitcast_fusion
  190.2 6.9 %all-to-all-start.3 = ((f32[16,8,128]{2,0,1:T(8,128)}), f32[16,8,128]{2,0,1:T(8,128)S(1)}, u32[]{:S(2)}, u32[]{:S(2)}) async-start(f32[16,8,128]{2,0,1:T(8,128)} %copy_bitcast_fusion), calls=%async_computation.3 | async-start | bytes 131072 | tf_op jit(solution)/shard_map/all_to_all | solution.py:74
  197.1 0.7 multiply_reduce_fusion
  197.8 8.1 %psum.35 = f32[]{:T(128)} all-reduce(f32[]{:T(128)} %multiply_reduce_fusion), channel_id=1, replica_groups=mesh['dp_0'=4,'dp_1'=8,'dp_2'=2,'tp_0'=4,'tp_1'=2] {'dp_0'}, use_global_device_ids=true, to_apply=%region_2.0 | all-reduce | flops 1 | bytes 8 | tf_op jit(solution)/shard_map/psum | solution.py:42
  205.9 13.0 %psum.36 = f32[]{:T(128)} all-reduce(f32[]{:T(128)} %psum.35), channel_id=1, replica_groups=mesh['dp_0'=4,'dp_1'=8,'dp_2'=2,'tp_0'=4,'tp_1'=2] {'dp_1'}, use_global_device_ids=true, to_apply=%region_3.0 | all-reduce | flops 1 | bytes 8 | tf_op jit(solution)/shard_map/psum | solution.py:42
  218.9 4.8 %psum.37 = f32[]{:T(128)} all-reduce(f32[]{:T(128)} %psum.36), channel_id=1, replica_groups=mesh['dp_0'=4,'dp_1'=8,'dp_2'=2,'tp_0'=4,'tp_1'=2] {'dp_2'}, use_global_device_ids=true, to_apply=%region_4.0 | all-reduce | flops 1 | bytes 8 | tf_op jit(solution)/shard_map/psum | solution.py:42
  223.7 10.4 %psum.38 = f32[]{:T(128)} all-reduce(f32[]{:T(128)} %psum.37), channel_id=1, replica_groups=mesh['dp_0'=4,'dp_1'=8,'dp_2'=2,'tp_0'=4,'tp_1'=2] {'tp_0'}, use_global_device_ids=true, to_apply=%region_5.0 | all-reduce | flops 1 | bytes 8 | tf_op jit(solution)/shard_map/psum | solution.py:42
  234.0 12.0 %psum.39 = f32[]{:T(128)} all-reduce(f32[]{:T(128)} %psum.38), channel_id=1, replica_groups=mesh['dp_0'=4,'dp_1'=8,'dp_2'=2,'tp_0'=4,'tp_1'=2] {'tp_1'}, use_global_device_ids=true, to_apply=%region_6.0 | all-reduce | flops 1 | bytes 8 | tf_op jit(solution)/shard_map/psum | solution.py:42
  246.8 0.0 all-to-all-done.3
  246.8 0.6 broadcast_multiply_fusion
Async XLA Ops:
  6.1 10.5 %copy-start = (bf16[1024,128]{1,0:T(8,128)(2,1)S(1)}, bf16[1024,128]{1,0:T(8,128)(2,1)}, u32[]{:S(2)}) copy-start(bf16[1024,128]{1,0:T(8,128)(2,1)} %param.5) | copy-start | bytes 786436
  6.1 59.3 %all-to-all-start = ((bf16[128,64,8,16]{0,3,1,2:T(8,128)(2,1)}), bf16[128,64,8,16]{0,3,1,2:T(8,128)(2,1)S(1)}, u32[]{:S(2)}, u32[]{:S(2)}) async-start(bf16[128,64,8,16]{0,3,1,2:T(8,128)(2,1)} %copy.13), calls=%async_computation | async-start | bytes 4194304 | tf_op jit(solution)/shard_map/all_to_all | solution.py:65
  67.0 42.1 %all-to-all-start.1 = ((bf16[8,1024,128]{1,2,0:T(8,128)(2,1)}), bf16[8,1024,128]{1,2,0:T(8,128)(2,1)}, u32[]{:S(2)}, u32[]{:S(2)}) async-start(bf16[8,1024,128]{1,2,0:T(8,128)(2,1)} %broadcast_in_dim.4), calls=%async_computation.1 | async-start | bytes 4194304 | tf_op jit(solution)/shard_map/all_to_all | solution.py:14
  190.2 56.5 %all-to-all-start.3 = ((f32[16,8,128]{2,0,1:T(8,128)}), f32[16,8,128]{2,0,1:T(8,128)S(1)}, u32[]{:S(2)}, u32[]{:S(2)}) async-start(f32[16,8,128]{2,0,1:T(8,128)} %copy_bitcast_fusion), calls=%async_computation.3 | async-start | bytes 131072 | tf_op jit(solution)/shard_map/all_to_all | solution.py:74
where the time goes:
time: 248 us; the launch traced here: 247 us
  blocking collectives  124 us (50%)
  waiting for transfers between devices  82.1 us (33%)
  starting transfers between devices  22.3 us (9%)
  local copies, waits for them, and re-layouts  11.1 us (4%)
  matrix products  4.58 us (2%)
  other arithmetic  2.82 us (1%)
    all_to_all x1, blocking collectives, sent_and_summed(): lax.all_to_all(pieces, axis, split_axis=0, concat_axis=0, tiled=True)  75.6 us
    all_to_all x1, waiting for transfers between devices, body(): lax.all_to_all(inputs, TP, split_axis=2, concat_axis=0, tiled=True)  48.7 us
    psum x5, blocking collectives, over_axes(): shard = lax.psum(shard, axis)  48.2 us
    all_to_all x1, waiting for transfers between devices, copy_for_each(): return lax.all_to_all(copies, axis, split_axis=0, concat_axis=0, tiled=True)  33.4 us
    all_to_all x1, starting transfers between devices, body(): lax.all_to_all(inputs, TP, split_axis=2, concat_axis=0, tiled=True)  10.5 us
    all_to_all x1, starting transfers between devices, body(): local = lax.all_to_all(summed, TP, split_axis=1, concat_axis=0, tiled=True)  6.87 us
    all_to_all x1, starting transfers between devices, copy_for_each(): return lax.all_to_all(copies, axis, split_axis=0, concat_axis=0, tiled=True)  4.97 us
  transfers between devices with their start and end apart: 3, of which 2 were waited for; matrix products, arithmetic and copies ran while one was open for 2% of the time, Pallas kernels for 0%

commit v1 on v0

--- a/solution.py
+++ b/solution.py
@@ -7,6 +7,12 @@
 DP = ("dp_0", "dp_1", "dp_2")
 TP = ("tp_0", "tp_1")
 DP_TP = ("dp_0", "dp_1", "dp_2", "tp_0", "tp_1")
+
+
+def gather_and_add(x, axis):
+    shards = lax.all_gather(x, axis, axis=0, tiled=False)
+    total = shards.sum(axis=0)
+    return total
 
 
 def copy_for_each(shard, axis):
@@ -39,7 +45,7 @@
 
 def over_axes(shard, axes):
     for axis in axes:
-        shard = lax.psum(shard, axis)
+        shard = gather_and_add(shard, axis)
     return shard
 
 

time: 248 us -> 261 us (1.052)
  blocking collectives: 124 us -> 44.7 us
  waiting for transfers between devices: 82.1 us -> 129 us
  starting transfers between devices: 22.3 us -> 50.2 us
  local copies, waits for them, and re-layouts: 11.1 us -> 24.2 us
  other arithmetic: 2.82 us -> 5.43 us
    all_to_all x1 -> x0, blocking collectives: 75.6 us -> none  [sent_and_summed(): lax.all_to_all(pieces, axis, split_axis=0, concat_axis=0, tiled=True)]
    psum x5 -> x0, blocking collectives: 48.2 us -> none  [over_axes(): shard = lax.psum(shard, axis)]
    all_to_all x0 -> x1, waiting for transfers between devices: none -> 46.5 us  [sent_and_summed(): lax.all_to_all(pieces, axis, split_axis=0, concat_axis=0, tiled=True)]
    unnamed x0 -> x5, blocking collectives: none -> 44.7 us
    all_to_all x0 -> x1, starting transfers between devices: none -> 27.9 us  [sent_and_summed(): lax.all_to_all(pieces, axis, split_axis=0, concat_axis=0, tiled=True)]
    unnamed x4 -> x21, local copies, waits for them, and re-layouts: 3.36 us -> 16.5 us
    reduce_sum x0 -> x5, other arithmetic: none -> 3.42 us  [gather_and_add(): total = shards.sum(axis=0)]
  transfers between devices with their start and end apart: 3 -> 4, of which waited for: 2 -> 3; matrix products, arithmetic and copies ran while one was open for 2% -> 8% of each run, Pallas kernels for 0% -> 0%
where the time goes in v1:
time: 261 us; the launch traced here: 260 us
  waiting for transfers between devices  129 us (49%)
  starting transfers between devices  50.2 us (19%)
  blocking collectives  44.7 us (17%)
  local copies, waits for them, and re-layouts  24.2 us (9%)
  matrix products  5.92 us (2%)
  other arithmetic  5.43 us (2%)
    all_to_all x1, waiting for transfers between devices, body(): lax.all_to_all(inputs, TP, split_axis=2, concat_axis=0, tiled=True)  48.7 us
    all_to_all x1, waiting for transfers between devices, sent_and_summed(): lax.all_to_all(pieces, axis, split_axis=0, concat_axis=0, tiled=True)  46.5 us
    unnamed x5, blocking collectives  44.7 us
    all_to_all x1, waiting for transfers between devices, copy_for_each(): return lax.all_to_all(copies, axis, split_axis=0, concat_axis=0, tiled=True)  33.4 us
    all_to_all x1, starting transfers between devices, sent_and_summed(): lax.all_to_all(pieces, axis, split_axis=0, concat_axis=0, tiled=True)  27.9 us
    unnamed x21, local copies, waits for them, and re-layouts  16.5 us
    all_to_all x1, starting transfers between devices, body(): lax.all_to_all(inputs, TP, split_axis=2, concat_axis=0, tiled=True)  10.5 us
    all_to_all x1, starting transfers between devices, body(): local = lax.all_to_all(summed, TP, split_axis=1, concat_axis=0, tiled=True)  6.87 us
  transfers between devices with their start and end apart: 4, of which 3 were waited for; matrix products, arithmetic and copies ran while one was open for 8% of the time, Pallas kernels for 0%

profile of v1, /device:TPU:1, one launch (start us, length us, event | category | flops | bytes accessed | tf_op | source)
XLA Modules:
  0.0 259.9 jit_solution(656903706584573158)
XLA Ops:
  0.0 0.0 copy-start.1
  0.0 3.2 %copy.12 = bf16[128,8192]{0,1:T(8,128)(2,1)S(1)} copy(bf16[128,8192]{1,0:T(8,128)(2,1)} %param.3) | data formatting | bytes 4194304 | tf_op args[0]
  3.2 0.0 copy-done.1
  3.3 0.4 fusion
  3.7 1.7 copy.13
  5.4 0.0 copy-start
  5.4 10.5 %all-to-all-start = ((bf16[128,64,8,16]{0,3,1,2:T(8,128)(2,1)}), bf16[128,64,8,16]{0,3,1,2:T(8,128)(2,1)S(1)}, u32[]{:S(2)}, u32[]{:S(2)}) async-start(bf16[128,64,8,16]{0,3,1,2:T(8,128)(2,1)} %copy.13), calls=%async_computation | async-start | bytes 4194304 | tf_op jit(solution)/shard_map/all_to_all | solution.py:71
  15.9 0.0 copy-done
  15.9 0.1 copy.15
  16.0 48.7 %all-to-all-done = bf16[128,64,8,16]{0,3,1,2:T(8,128)(2,1)S(1)} async-done(((bf16[128,64,8,16]{0,3,1,2:T(8,128)(2,1)}), bf16[128,64,8,16]{0,3,1,2:T(8,128)(2,1)S(1)}, u32[]{:S(2)}, u32[]{:S(2)}) %all-to-all-start) | async-done | bytes 2097184 | tf_op jit(solution)/shard_map/all_to_all | solution.py:71
  64.7 1.6 broadcast_in_dim.4
  66.3 5.0 %all-to-all-start.1 = ((bf16[8,1024,128]{1,2,0:T(8,128)(2,1)}), bf16[8,1024,128]{1,2,0:T(8,128)(2,1)}, u32[]{:S(2)}, u32[]{:S(2)}) async-start(bf16[8,1024,128]{1,2,0:T(8,128)(2,1)} %broadcast_in_dim.4), calls=%async_computation.1 | async-start | bytes 4194304 | tf_op jit(solution)/shard_map/all_to_all | solution.py:20
  71.3 3.7 %copy.14 = bf16[8,128,64,1,16]{1,0,4,2,3:T(8,128)(2,1)} copy(bf16[8,128,64,1,16]{1,4,2,0,3:T(8,128)(2,1)S(1)} %bitcast.40) | data formatting | bytes 4194304 | tf_op jit(solution)/shard_map/all_to_all | solution.py:71
  75.0 33.4 %all-to-all-done.1 = bf16[8,1024,128]{1,2,0:T(8,128)(2,1)} async-done(((bf16[8,1024,128]{1,2,0:T(8,128)(2,1)}), bf16[8,1024,128]{1,2,0:T(8,128)(2,1)}, u32[]{:S(2)}, u32[]{:S(2)}) %all-to-all-start.1) | async-done | bytes 2097184 | tf_op jit(solution)/shard_map/all_to_all | solution.py:20
  108.4 5.9 %fusion.4 = bf16[1024,1024]{1,0:T(8,128)(2,1)} fusion(bf16[1024,1024]{0,1:T(8,128)(2,1)} %bitcast.5, bf16[128,8,8,128]{3,2,1,0:T(8,128)(2,1)} %bitcast.43), kind=kOutput, calls=%fused_computation.6 | convolution fusion | flops 2148532224 | bytes 6291456 | tf_op jit(solution)/shard_map/dot_general | solution.py:73
  114.4 27.9 %all-to-all-start.2 = ((bf16[64,16,1024]{2,1,0:T(8,128)(2,1)}), bf16[64,16,1024]{2,1,0:T(8,128)(2,1)S(1)}, u32[]{:S(2)}, u32[]{:S(2)}) async-start(bf16[64,16,1024]{2,1,0:T(8,128)(2,1)} %bitcast.42), calls=%async_computation.2 | async-start | bytes 4194304 | tf_op jit(solution)/shard_map/all_to_all | solution.py:42
  142.3 1.3 dynamic-slice
  143.6 46.5 %all-to-all-done.2 = bf16[64,16,1024]{2,1,0:T(8,128)(2,1)S(1)} async-done(((bf16[64,16,1024]{2,1,0:T(8,128)(2,1)}), bf16[64,16,1024]{2,1,0:T(8,128)(2,1)S(1)}, u32[]{:S(2)}, u32[]{:S(2)}) %all-to-all-start.2) | async-done | bytes 2097184 | tf_op jit(solution)/shard_map/all_to_all | solution.py:42
  190.1 0.4 convert_reduce_fusion
  190.5 0.6 copy_bitcast_fusion
  191.1 6.9 %all-to-all-start.3 = ((f32[16,8,128]{2,0,1:T(8,128)}), f32[16,8,128]{2,0,1:T(8,128)S(1)}, u32[]{:S(2)}, u32[]{:S(2)}) async-start(f32[16,8,128]{2,0,1:T(8,128)} %copy_bitcast_fusion), calls=%async_computation.3 | async-start | bytes 131072 | tf_op jit(solution)/shard_map/all_to_all | solution.py:80
  198.0 0.6 multiply_reduce_fusion
  198.6 1.4 dynamic-update-slice
  200.0 1.3 dynamic-slice.1
  201.2 7.1 %all-reduce = f32[4]{0:T(128)S(1)} all-reduce(f32[4]{0:T(128)S(1)} %dynamic-update-slice), channel_id=1, replica_groups=mesh['dp_0'=4,'dp_1'=8,'dp_2'=2,'tp_0'=4,'tp_1'=2] {'dp_0'}, use_global_device_ids=true, to_apply=%add | all-reduce | flops 4 | bytes 32
  208.3 0.7 reduce_sum.65
  209.0 1.4 dynamic-update-slice.1
  210.4 1.3 dynamic-slice.2
  211.6 12.0 %all-reduce.1 = f32[8]{0:T(128)S(1)} all-reduce(f32[8]{0:T(128)S(1)} %dynamic-update-slice.1), channel_id=1, replica_groups=mesh['dp_0'=4,'dp_1'=8,'dp_2'=2,'tp_0'=4,'tp_1'=2] {'dp_1'}, use_global_device_ids=true, to_apply=%add.1 | all-reduce | flops 8 | bytes 64
  223.6 0.7 reduce_sum.66
  224.3 1.4 dynamic-update-slice.2
  225.7 1.3 dynamic-slice.3
  226.9 3.8 %all-reduce.2 = f32[2]{0:T(128)S(1)} all-reduce(f32[2]{0:T(128)S(1)} %dynamic-update-slice.2), channel_id=1, replica_groups=mesh['dp_0'=4,'dp_1'=8,'dp_2'=2,'tp_0'=4,'tp_1'=2] {'dp_2'}, use_global_device_ids=true, to_apply=%add.2 | all-reduce | flops 2 | bytes 16
  230.8 0.7 reduce_sum.67
  231.5 1.4 dynamic-update-slice.3
  232.8 1.3 dynamic-slice.4
  234.1 10.4 %all-reduce.3 = f32[4]{0:T(128)S(1)} all-reduce(f32[4]{0:T(128)S(1)} %dynamic-update-slice.3), channel_id=1, replica_groups=mesh['dp_0'=4,'dp_1'=8,'dp_2'=2,'tp_0'=4,'tp_1'=2] {'tp_0'}, use_global_device_ids=true, to_apply=%add.3 | all-reduce | flops 4 | bytes 32
  244.5 0.7 reduce_sum.68
  245.2 1.4 dynamic-update-slice.4
  246.5 11.3 %all-reduce.4 = f32[2]{0:T(128)S(1)} all-reduce(f32[2]{0:T(128)S(1)} %dynamic-update-slice.4), channel_id=1, replica_groups=mesh['dp_0'=4,'dp_1'=8,'dp_2'=2,'tp_0'=4,'tp_1'=2] {'tp_1'}, use_global_device_ids=true, to_apply=%add.4 | all-reduce | flops 2 | bytes 16
  257.8 0.7 reduce_sum.69
  259.2 0.0 all-to-all-done.3
  259.2 0.6 broadcast_multiply_fusion
  (6 shorter events, 0.0 us)
Async XLA Ops:
  0.0 3.2 %copy-start.1 = (bf16[128,64]{0,1:T(8,128)(2,1)S(1)}, bf16[128,64]{0,1:T(8,128)(2,1)}, u32[]{:S(2)}) copy-start(bf16[128,64]{0,1:T(8,128)(2,1)} %param.4) | copy-start | bytes 49156
  5.4 10.5 %copy-start = (bf16[1024,128]{1,0:T(8,128)(2,1)S(1)}, bf16[1024,128]{1,0:T(8,128)(2,1)}, u32[]{:S(2)}) copy-start(bf16[1024,128]{1,0:T(8,128)(2,1)} %param.5) | copy-start | bytes 786436
  5.4 59.3 %all-to-all-start = ((bf16[128,64,8,16]{0,3,1,2:T(8,128)(2,1)}), bf16[128,64,8,16]{0,3,1,2:T(8,128)(2,1)S(1)}, u32[]{:S(2)}, u32[]{:S(2)}) async-start(bf16[128,64,8,16]{0,3,1,2:T(8,128)(2,1)} %copy.13), calls=%async_computation | async-start | bytes 4194304 | tf_op jit(solution)/shard_map/all_to_all | solution.py:71
  66.3 42.1 %all-to-all-start.1 = ((bf16[8,1024,128]{1,2,0:T(8,128)(2,1)}), bf16[8,1024,128]{1,2,0:T(8,128)(2,1)}, u32[]{:S(2)}, u32[]{:S(2)}) async-start(bf16[8,1024,128]{1,2,0:T(8,128)(2,1)} %broadcast_in_dim.4), calls=%async_computation.1 | async-start | bytes 4194304 | tf_op jit(solution)/shard_map/all_to_all | solution.py:20
  114.4 75.8 %all-to-all-start.2 = ((bf16[64,16,1024]{2,1,0:T(8,128)(2,1)}), bf16[64,16,1024]{2,1,0:T(8,128)(2,1)S(1)}, u32[]{:S(2)}, u32[]{:S(2)}) async-start(bf16[64,16,1024]{2,1,0:T(8,128)(2,1)} %bitcast.42), calls=%async_computation.2 | async-start | bytes 4194304 | tf_op jit(solution)/shard_map/all_to_all | solution.py:42
  191.1 68.1 %all-to-all-start.3 = ((f32[16,8,128]{2,0,1:T(8,128)}), f32[16,8,128]{2,0,1:T(8,128)S(1)}, u32[]{:S(2)}, u32[]{:S(2)}) async-start(f32[16,8,128]{2,0,1:T(8,128)} %copy_bitcast_fusion), calls=%async_computation.3 | async-start | bytes 131072 | tf_op jit(solution)/shard_map/all_to_all | solution.py:80
